TPU v7x, 32 devices: a whole 2x2x4 slice. The times are simulated.
32 devices in a mesh: fsdp: 16 (over z, y, core), sp: 2 (over x).
Axes of the slice: x: 2, y: 2, z: 4, core: 2. Of those that a mesh axis runs over, the one named last changes fastest.
Arguments:
- latents: bfloat16 [32, 256, 768], P('fsdp', 'sp'), may hold values from -6 to 6
- condition: bfloat16 [32, 768], P('fsdp'), may hold values from -6 to 6
- cotangent: bfloat16 [32, 256, 768], P('fsdp', 'sp'), may hold values from -6 to 6
- w_ada: bfloat16 [768, 4608], P('fsdp'), may hold values from -0.21875 to 0.21875
- b_ada: bfloat16 [4608], P('fsdp'), may hold values from -3 to 3
- w_qkv: bfloat16 [768, 2304], P('fsdp'), may hold values from -0.21875 to 0.21875
- b_query: bfloat16 [768], P('fsdp'), may hold values from -3 to 3
- b_value: bfloat16 [768], P('fsdp'), may hold values from -3 to 3
- w_out: bfloat16 [768, 768], P('fsdp'), may hold values from -0.875 to 0.875
- b_out: bfloat16 [768], P('fsdp'), may hold values from -3 to 3
- w_up: bfloat16 [768, 3072], P('fsdp'), may hold values from -0.21875 to 0.21875
- b_up: bfloat16 [3072], P('fsdp'), may hold values from -3 to 3
- w_down: bfloat16 [3072, 768], P('fsdp'), may hold values from -0.109375 to 0.109375
- b_down: bfloat16 [768], P('fsdp'), may hold values from -3 to 3
Outputs:
- output: bfloat16 [32, 256, 768], P('fsdp', 'sp')
- grad_latents: float32 [32, 256, 768], P('fsdp', 'sp')
- grad_condition: float32 [32, 768], P('fsdp')
- grad_w_ada: float32 [768, 4608], P(('fsdp', 'sp'))
- grad_b_ada: float32 [4608], P(('fsdp', 'sp'))
- grad_w_qkv: float32 [768, 2304], P(('fsdp', 'sp'))
- grad_b_query: float32 [768], P(('fsdp', 'sp'))
- grad_b_value: float32 [768], P(('fsdp', 'sp'))
- grad_w_out: float32 [768, 768], P(('fsdp', 'sp'))
- grad_b_out: float32 [768], P(('fsdp', 'sp'))
- grad_w_up: float32 [768, 3072], P(('fsdp', 'sp'))
- grad_b_up: float32 [3072], P(('fsdp', 'sp'))
- grad_w_down: float32 [3072, 768], P(('fsdp', 'sp'))
- grad_b_down: float32 [768], P(('fsdp', 'sp'))
All inputs are finite; a program needn't handle non-finite values.
Results may differ from a plain program's by a relative error of at most 0.015.
The roundings to bfloat16 on the way count: a program that leaves them out, or rounds other values in their place, can miss the bound.
Values may be sent and summed in bfloat16 or wider, within the bound.
A program may use at most 256 MiB of HBM per device.

v0:
```python
import jax
import jax.numpy as jnp
from jax import lax
from jax.sharding import PartitionSpec as P

D = 768
H = 12
HD = 64
eps = 1e-06


def normalize(values):
    centered = values - jnp.mean(values, axis=-1, keepdims=True)
    inverse = lax.rsqrt(jnp.mean(centered * centered, axis=-1, keepdims=True) + eps)
    return (centered * inverse, inverse)


def norm_back(grad_in, normed, inverse):
    return inverse * (
        grad_in
        - jnp.mean(grad_in, axis=-1, keepdims=True)
        - normed * jnp.mean(grad_in * normed, axis=-1, keepdims=True)
    )


def gelu_tanh(values):
    return jax.nn.gelu(values, approximate=True)


def silu_back(values, grad_out):
    return jax.vjp(jax.nn.silu, values)[1](grad_out)[0]


def gelu_back(values, grad_out):
    return jax.vjp(gelu_tanh, values)[1](grad_out)[0]


LANES = 2048


def body(
    latents,
    condition,
    cotangent,
    w_ada,
    b_ada,
    w_qkv,
    b_query,
    b_value,
    w_out,
    b_out,
    w_up,
    b_up,
    w_down,
    b_down,
):
    f32 = jnp.float32
    bf16 = jnp.bfloat16
    fsdp_count = lax.axis_size("fsdp")
    sp_count = lax.axis_size("sp")
    owners = fsdp_count * sp_count
    fsdp_index = lax.axis_index("fsdp")
    sp_index = lax.axis_index("sp")
    owner_index = fsdp_index * sp_count + sp_index
    pair_latents = latents.shape[0]
    own_latents = pair_latents // sp_count
    latent_total = pair_latents * fsdp_count
    tokens_all = latents.shape[1] * sp_count
    scale_factor = HD ** (-0.5)
    small = [condition.reshape(-1), b_ada, b_query, b_value, b_out, b_up, b_down]
    width = sum((part.size for part in small))
    padded = -(-width // LANES) * LANES
    small.append(jnp.zeros((padded - width,), bf16))
    small_all = lax.all_gather(
        jnp.concatenate(small).reshape(1, padded // 128, 128), "fsdp", axis=0, tiled=True
    ).reshape(fsdp_count, padded)
    pieces = []
    start = 0
    for part in small[:-1]:
        pieces.append(small_all[:, start : start + part.size].reshape(-1))
        start = start + part.size
    cond_all, ada_bias, query_bias, value_bias, out_bias, up_bias, down_bias = pieces
    cond_all = cond_all.reshape(latent_total, D).astype(f32)
    silu_all = jax.nn.silu(cond_all)
    inputs = lax.all_to_all(latents, "sp", split_axis=0, concat_axis=1, tiled=True).astype(f32)
    grad_out = lax.all_to_all(cotangent, "sp", split_axis=0, concat_axis=1, tiled=True).astype(f32)
    ada_rows = w_ada.shape[0]
    silu_mine = lax.dynamic_index_in_dim(
        silu_all.astype(bf16).reshape(fsdp_count, sp_count, own_latents, D), sp_index, 1, False
    )
    silu_mine = lax.dynamic_index_in_dim(
        silu_mine.reshape(fsdp_count * own_latents, fsdp_count, ada_rows), fsdp_index, 1, False
    )
    mod_part = jnp.dot(silu_mine, w_ada, preferred_element_type=f32)
    mod_part = lax.all_to_all(
        mod_part.reshape(fsdp_count, own_latents * 6 * D),
        "fsdp",
        split_axis=0,
        concat_axis=0,
        tiled=True,
    )
    modulate = jnp.sum(mod_part, axis=0).reshape(own_latents, 6 * D) + ada_bias.astype(f32)
    mod_parts = modulate.reshape(own_latents, 6, 1, D)
    shift_one, scale_one, gate_one = (mod_parts[:, 0], mod_parts[:, 1], mod_parts[:, 2])
    shift_two, scale_two, gate_two = (mod_parts[:, 3], mod_parts[:, 4], mod_parts[:, 5])
    qkv_full = lax.all_gather(w_qkv, "fsdp", axis=0, tiled=True)
    out_full = lax.all_gather(w_out, "fsdp", axis=0, tiled=True)
    up_full = lax.all_gather(w_up, "fsdp", axis=0, tiled=True)
    down_full = lax.all_gather(w_down, "fsdp", axis=0, tiled=True)
    normed_one, inverse_one = normalize(inputs)
    attn_in = (normed_one * (1.0 + scale_one) + shift_one).astype(bf16)
    qkv_bias = jnp.concatenate([query_bias, jnp.zeros_like(query_bias), value_bias]).astype(f32)
    projected = (
        jnp.einsum("btd,de->bte", attn_in, qkv_full, preferred_element_type=f32) + qkv_bias
    ).astype(bf16)
    heads = projected.reshape(own_latents, tokens_all, 3, H, HD).transpose(2, 0, 3, 1, 4)
    queries, key_heads, value_heads = (heads[0], heads[1], heads[2])
    scores = (
        jnp.einsum("bhqd,bhkd->bhqk", queries, key_heads, preferred_element_type=f32) * scale_factor
    )
    log_total = jnp.log(jnp.sum(jnp.exp(scores), axis=-1, keepdims=True))
    soft_float = jnp.exp(scores - log_total)
    soft_half = soft_float.astype(bf16)
    mixed = jnp.einsum(
        "bhqk,bhkd->bhqd", soft_half, value_heads, preferred_element_type=f32
    ).astype(bf16)
    mixed_tokens = mixed.transpose(0, 2, 1, 3).reshape(own_latents, tokens_all, D)
    attn_proj = jnp.einsum(
        "btd,de->bte", mixed_tokens, out_full, preferred_element_type=f32
    ) + out_bias.astype(f32)
    residual = inputs + gate_one * attn_proj
    normed_two, inverse_two = normalize(residual)
    mlp_in = (normed_two * (1.0 + scale_two) + shift_two).astype(bf16)
    up_value = jnp.einsum(
        "btd,df->btf", mlp_in, up_full, preferred_element_type=f32
    ) + up_bias.astype(f32)
    activated = gelu_tanh(up_value).astype(bf16)
    down_value = jnp.einsum(
        "btf,fd->btd", activated, down_full, preferred_element_type=f32
    ) + down_bias.astype(f32)
    output = (residual + gate_two * down_value).astype(bf16)
    output = lax.all_to_all(output, "sp", split_axis=1, concat_axis=0, tiled=True)
    grad_gate_two = jnp.sum(grad_out * down_value, axis=1)
    grad_down = (grad_out * gate_two).astype(bf16)
    gw_down = jnp.einsum("btf,btd->fd", activated, grad_down, preferred_element_type=f32)
    gb_down = jnp.sum(grad_down.astype(f32), axis=(0, 1))
    grad_act = jnp.einsum("btd,fd->btf", grad_down, down_full, preferred_element_type=f32)
    grad_up = gelu_back(up_value, grad_act).astype(bf16)
    gw_up = jnp.einsum("btd,btf->df", mlp_in, grad_up, preferred_element_type=f32)
    gb_up = jnp.sum(grad_up.astype(f32), axis=(0, 1))
    grad_mlp = jnp.einsum("btf,df->btd", grad_up, up_full, preferred_element_type=f32)
    grad_scale_two = jnp.sum(grad_mlp * normed_two, axis=1)
    grad_shift_two = jnp.sum(grad_mlp, axis=1)
    grad_resid = grad_out + norm_back(grad_mlp * (1.0 + scale_two), normed_two, inverse_two)
    grad_gate_one = jnp.sum(grad_resid * attn_proj, axis=1)
    grad_proj = (grad_resid * gate_one).astype(bf16)
    gw_out = jnp.einsum("btd,bte->de", mixed_tokens, grad_proj, preferred_element_type=f32)
    gb_out = jnp.sum(grad_proj.astype(f32), axis=(0, 1))
    grad_mixed = jnp.einsum("bte,de->btd", grad_proj, out_full, preferred_element_type=f32).astype(
        bf16
    )
    grad_heads = grad_mixed.reshape(own_latents, tokens_all, H, HD).transpose(0, 2, 1, 3)
    grad_soft = jnp.einsum("bhqd,bhkd->bhqk", grad_heads, value_heads, preferred_element_type=f32)
    delta_sum = jnp.sum(soft_float * grad_soft, axis=-1, keepdims=True)
    grad_scores = (soft_float * (grad_soft - delta_sum)).astype(bf16)
    grad_queries = (
        jnp.einsum("bhqk,bhkd->bhqd", grad_scores, key_heads, preferred_element_type=f32)
        * scale_factor
    ).astype(bf16)
    grad_keys = (
        jnp.einsum("bhqk,bhqd->bhkd", grad_scores, queries, preferred_element_type=f32)
        * scale_factor
    ).astype(bf16)
    grad_values = jnp.einsum(
        "bhqk,bhqd->bhkd", soft_half, grad_heads, preferred_element_type=f32
    ).astype(bf16)
    grad_tokens = (
        jnp.stack([grad_queries, grad_keys, grad_values], axis=0)
        .transpose(1, 3, 0, 2, 4)
        .reshape(own_latents, tokens_all, 3 * D)
    )
    gw_qkv = jnp.einsum("btd,bte->de", attn_in, grad_tokens, preferred_element_type=f32)
    grad_tok_float = grad_tokens.astype(f32)
    gb_query = jnp.sum(grad_tok_float[:, :, :D], axis=(0, 1))
    gb_value = jnp.sum(grad_tok_float[:, :, 2 * D :], axis=(0, 1))
    grad_attn_in = jnp.einsum("bte,de->btd", grad_tokens, qkv_full, preferred_element_type=f32)
    grad_scale_one = jnp.sum(grad_attn_in * normed_one, axis=1)
    grad_shift_one = jnp.sum(grad_attn_in, axis=1)
    grad_latents = grad_resid + norm_back(grad_attn_in * (1.0 + scale_one), normed_one, inverse_one)
    grad_latents = lax.all_to_all(grad_latents, "sp", split_axis=1, concat_axis=0, tiled=True)
    grad_mod = jnp.concatenate(
        [
            grad_shift_one,
            grad_scale_one,
            grad_gate_one,
            grad_shift_two,
            grad_scale_two,
            grad_gate_two,
        ],
        axis=1,
    )
    grad_mod = lax.all_to_all(
        jnp.broadcast_to(grad_mod[None], (owners, own_latents, 6 * D)),
        ("fsdp", "sp"),
        split_axis=0,
        concat_axis=0,
        tiled=True,
    ).reshape(latent_total, 6 * D)
    rows = D // owners
    biases = (gb_query, gb_value, gb_out, gb_up, gb_down)
    bias_rows = jnp.concatenate([part.reshape(owners, -1) for part in biases], axis=1)
    bias_width = bias_rows.shape[1]
    bias_lanes = -(-bias_width // (rows * 128)) * 128
    bias_rows = jnp.pad(bias_rows, ((0, 0), (0, rows * bias_lanes - bias_width)))
    stack = down_full.shape[0] // D
    gw_down = (
        gw_down.astype(bf16)
        .reshape(owners, stack, rows, D)
        .transpose(0, 2, 1, 3)
        .reshape(D, stack * D)
    )
    packed = jnp.concatenate(
        [
            gw_down,
            gw_up.astype(bf16),
            gw_qkv.astype(bf16),
            gw_out.astype(bf16),
            bias_rows.astype(bf16).reshape(D, bias_lanes),
        ],
        axis=1,
    )
    owned = lax.psum_scatter(packed, ("fsdp", "sp"), scatter_dimension=0, tiled=True).astype(f32)
    own_weights = []
    start = 0
    for width in (stack * D, up_full.shape[1], 3 * D, D, bias_lanes):
        own_weights.append(owned[:, start : start + width])
        start = start + width
    own_down, own_up, own_qkv, own_out, bias_sums = own_weights
    own_down = own_down.reshape(rows, stack, D).transpose(1, 0, 2).reshape(stack * rows, D)
    bias_sums = bias_sums.reshape(-1)
    own_bias = []
    start = 0
    for part in biases:
        width = part.size // owners
        own_bias.append(bias_sums[start : start + width])
        start = start + width
    own_gb_query, own_gb_value, own_gb_out, own_gb_up, own_gb_down = own_bias
    silu_rows = lax.dynamic_index_in_dim(
        silu_all.reshape(latent_total, owners, D // owners), owner_index, 1, False
    )
    own_ada = jnp.dot(silu_rows.T, grad_mod, precision=lax.Precision.HIGHEST)
    own_gb_ada = lax.dynamic_index_in_dim(
        jnp.sum(grad_mod, axis=0).reshape(owners, -1), owner_index, 0, False
    )
    grad_silu = jnp.dot(grad_mod.astype(bf16), w_ada.T, preferred_element_type=f32)
    grad_silu = lax.all_to_all(
        grad_silu.reshape(fsdp_count, pair_latents * ada_rows),
        "fsdp",
        split_axis=0,
        concat_axis=0,
        tiled=True,
    )
    grad_silu = (
        grad_silu.reshape(fsdp_count, pair_latents, ada_rows)
        .transpose(1, 0, 2)
        .reshape(pair_latents, D)
    )
    grad_condition = silu_back(condition.astype(f32), grad_silu)
    return (
        output,
        grad_latents,
        grad_condition,
        own_ada,
        own_gb_ada,
        own_qkv,
        own_gb_query,
        own_gb_value,
        own_out,
        own_gb_out,
        own_up,
        own_gb_up,
        own_down,
        own_gb_down,
    )


def solution(mesh):
    in_specs = (
        P("fsdp", "sp", None),
        P("fsdp", None),
        P("fsdp", "sp", None),
        P("fsdp", None),
        P("fsdp"),
        P("fsdp", None),
        P("fsdp"),
        P("fsdp"),
        P("fsdp", None),
        P("fsdp"),
        P("fsdp", None),
        P("fsdp"),
        P("fsdp", None),
        P("fsdp"),
    )
    out_specs = (
        P("fsdp", "sp", None),
        P("fsdp", "sp", None),
        P("fsdp", None),
        P(("fsdp", "sp"), None),
        P(("fsdp", "sp")),
        P(("fsdp", "sp"), None),
        P(("fsdp", "sp")),
        P(("fsdp", "sp")),
        P(("fsdp", "sp"), None),
        P(("fsdp", "sp")),
        P(("fsdp", "sp"), None),
        P(("fsdp", "sp")),
        P(("fsdp", "sp"), None),
        P(("fsdp", "sp")),
    )
    return jax.shard_map(body, mesh=mesh, in_specs=in_specs, out_specs=out_specs, check_vma=False)
```

profile of v0, /device:TPU:0, one launch (start us, length us, event | category | flops | bytes accessed | tf_op | source)
XLA Modules:
  0.0 443.4 jit_solution(5523221434767197551)
XLA Ops:
  10.0 4.2 all-to-all-start
  14.9 4.1 concatenate.24
  19.1 22.7 %all_gather.15 = bf16[16,32,128]{2,1,0:T(8,128)(2,1)S(1)} all-gather(bf16[1,32,128]{2,1,0:T(8,128)(2,1)S(1)} %bitcast.188), channel_id=1, replica_groups=mesh['fsdp'=16,'sp'=2] {'fsdp'}, dimensions={0}, use_global_device_ids=true | all-gather | bytes 139264 | tf_op jit(solution)/shard_map/all_gather | solution.py:74
  43.7 3.5 all-to-all-start.1
  48.0 13.7 %all-to-all-done.1 = f32[16,1,4608]{2,1,0:T(1,128)S(1)} async-done(((f32[16,1,4608]{2,1,0:T(1,128)}), f32[16,1,4608]{2,1,0:T(1,128)S(1)}, u32[]{:S(2)}, u32[]{:S(2)}) %all-to-all-start.1) | async-done | bytes 294944 | tf_op jit(solution)/shard_map/all_to_all | solution.py:95
  61.7 3.8 all-to-all-start.3
  65.8 6.4 %all-to-all-done.3 = bf16[2,128,768]{2,1,0:T(8,128)(2,1)S(1)} async-done(((bf16[2,128,768]{2,1,0:T(8,128)(2,1)}), bf16[2,128,768]{2,1,0:T(8,128)(2,1)S(1)}, u32[]{:S(2)}, u32[]{:S(2)}) %all-to-all-start.3) | async-done | bytes 393248 | tf_op jit(solution)/shard_map/all_to_all | solution.py:86
  74.5 4.1 fusion.3
  78.6 1.6 copy.105
  80.2 2.4 fusion.60
  82.6 4.9 %convolution_convert_fusion.4 = bf16[12,256,64]{1,2,0:T(8,128)(2,1)} fusion(f32[12,256,256]{1,2,0:T(8,128)} %fusion.60, bf16[3,1,12,256,64]{3,4,2,1,0:T(8,128)(2,1)S(1)} %bitcast.160), kind=kOutput, calls=%fused_computation.34 | convolution fusion | flops 104008960 | bytes 7077888 | tf_op jit(solution)/shard_map/bhqk,bhkd->bhqd/dot_general | solution.py:124
  87.4 17.1 %all-gather.7.cloned.1.call-done = bf16[768,768]{1,0:T(8,128)(2,1)} async-done(((bf16[48,768]{1,0:T(8,128)(2,1)}), bf16[768,768]{1,0:T(8,128)(2,1)}) %all-gather.7.cloned.1.call-update) | async-done | bytes 1179664 | tf_op jit(solution)/shard_map/all_gather | solution.py:107
  104.6 2.8 fusion.83
  107.6 51.3 %all-gather.11.cloned.1.call-done = bf16[3072,768]{1,0:T(8,128)(2,1)} async-done(((bf16[192,768]{1,0:T(8,128)(2,1)}), bf16[3072,768]{1,0:T(8,128)(2,1)}) %all-gather.11.cloned.1.call-update) | async-done | bytes 4718608 | tf_op jit(solution)/shard_map/all_gather | solution.py:109
  158.9 5.6 %fusion.86 = f32[256,3072]{1,0:T(8,128)} fusion(bf16[256,768]{1,0:T(8,128)(2,1)} %fusion.24, bf16[3072,768]{1,0:T(8,128)(2,1)} %all-gather.11.cloned.1.call-done), kind=kOutput, calls=%fused_computation.159 | convolution fusion | flops 1207959552 | bytes 8257536 | tf_op jit(solution)/shard_map/btd,fd->btf/dot_general | solution.py:147
  164.5 48.2 %all-gather.9.cloned.1.call-done = bf16[768,3072]{1,0:T(8,128)(2,1)} async-done(((bf16[48,3072]{1,0:T(8,128)(2,1)}), bf16[768,3072]{1,0:T(8,128)(2,1)}) %all-gather.9.cloned.1.call-update) | async-done | bytes 4718608 | tf_op jit(solution)/shard_map/all_gather | solution.py:108
  212.7 7.0 %fusion.80 = (bf16[3072]{0:T(1024)(128)(2,1)S(1)}, bf16[256,3072]{1,0:T(8,128)(2,1)S(1)}, f32[256,3072]{1,0:T(8,128)S(1)}) fusion(f32[256,3072]{1,0:T(8,128)} %fusion.86, f32[3072]{0:T(1024)S(1)} %reshape.760, bf16[768,3072]{1,0:T(8,128)(2,1)} %all-gather.9.cloned.1.call-done, f32[256,768]{1,0:T(8,128)S(1)} %get-tuple-element.36, ...), kind=kOutput, calls=%fused_computation.153 | convolution fusion | flops 1226241024 | bytes 13395968 | tf_op jit(solution)/shard_map/btd,df->btf/dot_general | solution.py:134
  219.8 1.4 fusion.87
  222.1 1.7 copy-done.2
  223.8 2.9 fusion.25
  226.7 1.3 fusion.82
  230.2 5.0 %fusion.20 = bf16[1,1,12,256,64]{3,4,2,1,0:T(8,128)(2,1)} fusion(bf16[12,256,64]{1,2,0:T(8,128)(2,1)} %bitcast.174, f32[12,256,256]{1,2,0:T(8,128)} %fusion.60), kind=kOutput, calls=%fused_computation.39 | convolution fusion | flops 104008960 | bytes 3932160 | tf_op jit(solution)/shard_map/bhqk,bhqd->bhkd/dot_general | solution.py:174
  235.8 1.3 copy-done.1
  237.1 2.9 multiply_reduce_fusion
  240.6 1.4 fusion.22
  241.9 1.1 fusion.21
  243.1 4.4 convolution_convert_fusion.2
  247.7 1.2 pad_maximum_fusion
  249.8 4.7 %copy.117 = bf16[32,24,4,768]{3,2,1,0:T(4,128)(2,1)S(1)} copy(bf16[32,24,4,768]{3,1,2,0:T(8,128)(2,1)} %bitcast.167) | data formatting | bytes 9437184 | tf_op jit(solution)/shard_map/transpose | solution.py:219
  255.6 2.5 constant_dynamic-update-slice_fusion.7
  258.0 3.7 fusion.2
  261.8 2.9 fusion.1
  264.7 1.6 fusion.17
  269.1 3.3 reduce.65
  273.2 3.6 all-to-all-start.2
  276.8 3.9 fusion.39
  281.1 1.7 copy.113
  282.8 1.2 all-to-all-done.2
  284.0 3.6 all-to-all-start.4
  287.7 10.6 %all-to-all-done.4 = f32[1,256,768]{2,0,1:T(1,128)S(1)} async-done(((f32[1,256,768]{2,0,1:T(1,128)}), f32[1,256,768]{2,0,1:T(1,128)S(1)}, u32[]{:S(2)}, u32[]{:S(2)}) %all-to-all-start.4) | async-done | bytes 786464 | tf_op jit(solution)/shard_map/all_to_all | solution.py:190
  299.4 2.6 all-to-all-start.5
  304.5 18.4 %all-to-all-done.5 = f32[32,1,4608]{2,1,0:T(1,128)S(1)} async-done(((f32[32,1,4608]{2,1,0:T(1,128)}), f32[32,1,4608]{2,1,0:T(1,128)S(1)}, u32[]{:S(2)}, u32[]{:S(2)}) %all-to-all-start.5) | async-done | bytes 589856 | tf_op jit(solution)/shard_map/all_to_all | solution.py:202
  323.9 3.5 all-to-all-start.6
  327.8 1.3 fusion.46
  329.7 6.0 %all-to-all-done.6 = f32[16,1,96]{2,1,0:T(1,128)S(1)} async-done(((f32[16,1,96]{2,1,0:T(1,128)}), f32[16,1,96]{2,1,0:T(1,128)S(1)}, u32[]{:S(2)}, u32[]{:S(2)}) %all-to-all-start.6) | async-done | bytes 6176 | tf_op jit(solution)/shard_map/all_to_all | solution.py:256
  337.6 92.9 %reduce-scatter.4.cloned.1.call-done = bf16[24,9344]{1,0:T(8,128)(2,1)} async-done(((bf16[768,9344]{1,0:T(8,128)(2,1)}), bf16[24,9344]{1,0:T(8,128)(2,1)}) %reduce-scatter.4.cloned.1.call-update) | async-done | bytes 448528
  430.5 1.1 convert_element_type.313
  432.8 1.7 fusion.84
  (144 shorter events, 30.4 us)
Async XLA Ops:
  7.2 35.3 %copy-start = (bf16[48,4608]{1,0:T(8,128)(2,1)S(1)}, bf16[48,4608]{1,0:T(8,128)(2,1)}, u32[]{:S(2)}) copy-start(bf16[48,4608]{1,0:T(8,128)(2,1)} %param.17) | copy-start | bytes 1327108
  7.2 67.3 %all-gather.5.cloned.1.call-start = ((), (), s32[]{:S(2)}) async-start(), calls=%async_computation.8 | async-start | bytes 3760128 | tf_op jit(solution)/shard_map/all_gather | solution.py:106
  7.9 96.6 %all-gather.7.cloned.1.call-start = ((), (), s32[]{:S(2)}) async-start(), calls=%async_computation.9 | async-start | bytes 1253376 | tf_op jit(solution)/shard_map/all_gather | solution.py:107
  8.7 150.2 %all-gather.11.cloned.1.call-start = ((), (), s32[]{:S(2)}) async-start(), calls=%async_computation.11 | async-start | bytes 5013504 | tf_op jit(solution)/shard_map/all_gather | solution.py:109
  9.4 203.3 %all-gather.9.cloned.1.call-start = ((), (), s32[]{:S(2)}) async-start(), calls=%async_computation.10 | async-start | bytes 5013504 | tf_op jit(solution)/shard_map/all_gather | solution.py:108
  10.0 33.7 %all-to-all-start = ((bf16[2,128,768]{2,1,0:T(8,128)(2,1)}), bf16[2,128,768]{2,1,0:T(8,128)(2,1)S(1)}, u32[]{:S(2)}, u32[]{:S(2)}) async-start(bf16[2,128,768]{2,1,0:T(8,128)(2,1)} %param.14), calls=%async_computation | async-start | bytes 786432 | tf_op jit(solution)/shard_map/all_to_all | solution.py:85
  43.7 18.0 %all-to-all-start.1 = ((f32[16,1,4608]{2,1,0:T(1,128)}), f32[16,1,4608]{2,1,0:T(1,128)S(1)}, u32[]{:S(2)}, u32[]{:S(2)}) async-start(f32[16,1,4608]{2,1,0:T(1,128)} %copy.104), calls=%async_computation.1 | async-start | bytes 589824 | tf_op jit(solution)/shard_map/all_to_all | solution.py:95
  61.7 10.5 %all-to-all-start.3 = ((bf16[2,128,768]{2,1,0:T(8,128)(2,1)}), bf16[2,128,768]{2,1,0:T(8,128)(2,1)S(1)}, u32[]{:S(2)}, u32[]{:S(2)}) async-start(bf16[2,128,768]{2,1,0:T(8,128)(2,1)} %param.16), calls=%async_computation.3 | async-start | bytes 786432 | tf_op jit(solution)/shard_map/all_to_all | solution.py:86
  65.5 365.0 %reduce-scatter.4.cloned.1.call-start = ((), (), s32[]{:S(2)}) async-start(), calls=%async_computation.12 | async-start | bytes 14800896
  212.7 7.0 %copy-start.16 = (bf16[768,3072]{1,0:T(8,128)(2,1)S(1)}, bf16[768,3072]{1,0:T(8,128)(2,1)}, u32[]{:S(2)}) copy-start(bf16[768,3072]{1,0:T(8,128)(2,1)} %all-gather.9.cloned.1.call-done) | copy-start | bytes 14155780
  219.7 1.5 copy-start.17
  219.8 2.4 copy-start.19
  219.8 4.0 copy-start.2
  226.7 2.0 copy-start.3
  228.0 0.8 copy-start.5
  230.2 5.0 %copy-start.12 = (bf16[256,768]{0,1:T(8,128)(2,1)S(1)}, bf16[256,768]{0,1:T(8,128)(2,1)}, u32[]{:S(2)}) copy-start(bf16[256,768]{0,1:T(8,128)(2,1)} %copy.109) | copy-start | bytes 1179652
  235.2 1.9 copy-start.1
  240.5 2.5 copy-start.9
  240.6 2.5 copy-start.20
  243.1 4.6 %copy-start.10 = (bf16[1,1,12,256,64]{3,4,2,1,0:T(8,128)(2,1)S(1)}, bf16[1,1,12,256,64]{3,4,2,1,0:T(8,128)(2,1)}, u32[]{:S(2)}) copy-start(bf16[1,1,12,256,64]{3,4,2,1,0:T(8,128)(2,1)} %fusion.22) | copy-start | bytes 1179652
  255.6 2.5 copy-start.18
  258.0 3.7 copy-start.13
  261.8 2.9 copy-start.6
  261.8 2.9 copy-start.11
  267.0 1.0 copy-start.14
  273.2 10.8 %all-to-all-start.2 = ((bf16[2,2,49152]{2,1,0:T(2,128)(2,1)}), bf16[2,2,49152]{2,1,0:T(2,128)(2,1)S(1)}, u32[]{:S(2)}, u32[]{:S(2)}) async-start(bf16[2,2,49152]{2,1,0:T(2,128)(2,1)} %reshape.781), calls=%async_computation.2 | async-start | bytes 786432 | tf_op jit(solution)/shard_map/all_to_all | solution.py:142
  276.8 4.0 copy-start.7
  276.8 4.0 copy-start.8
  284.0 14.2 %all-to-all-start.4 = ((f32[1,256,768]{2,0,1:T(1,128)}), f32[1,256,768]{2,0,1:T(1,128)S(1)}, u32[]{:S(2)}, u32[]{:S(2)}) async-start(f32[1,256,768]{2,0,1:T(1,128)} %copy.113), calls=%async_computation.4 | async-start | bytes 1572864 | tf_op jit(solution)/shard_map/all_to_all | solution.py:190
  299.4 23.6 %all-to-all-start.5 = ((f32[32,1,4608]{2,1,0:T(1,128)}), f32[32,1,4608]{2,1,0:T(1,128)S(1)}, u32[]{:S(2)}, u32[]{:S(2)}) async-start(f32[32,1,4608]{2,1,0:T(1,128)} %broadcast_in_dim.11), calls=%async_computation.5 | async-start | bytes 1179648 | tf_op jit(solution)/shard_map/all_to_all | solution.py:202
  302.4 34.6 %copy-start.15 = (bf16[2,768]{1,0:T(2,128)(2,1)S(1)}, bf16[2,768]{1,0:T(2,128)(2,1)}, u32[]{:S(2)}) copy-start(bf16[2,768]{1,0:T(2,128)(2,1)} %param.15) | copy-start | bytes 9220
  323.9 11.8 %all-to-all-start.6 = ((f32[16,1,96]{2,1,0:T(1,128)}), f32[16,1,96]{2,1,0:T(1,128)S(1)}, u32[]{:S(2)}, u32[]{:S(2)}) async-start(f32[16,1,96]{2,1,0:T(1,128)} %bitcast.29), calls=%async_computation.6 | async-start | bytes 16384 | tf_op jit(solution)/shard_map/all_to_all | solution.py:256
  430.5 5.0 %copy-start.4 = (bf16[24,9344]{1,0:T(8,128)(2,1)S(1)}, bf16[24,9344]{1,0:T(8,128)(2,1)}, u32[]{:S(2)}) copy-start(bf16[24,9344]{1,0:T(8,128)(2,1)} %reduce-scatter.4.cloned.1.call-done) | copy-start | bytes 1345540
Sparse Core Ops, SparseCore 0:
  10.3 55.0 all-gather.4
  67.7 36.8 all-gather.6
  106.9 51.9 all-gather.10
  161.0 51.6 all-gather.8
  267.1 163.3 reduce-scatter.3
where the time goes:
time: 444 us; the launch traced here: 443 us
  waiting for transfers between devices  268 us (60%)
  matrix products  58 us (13%)
  local copies, waits for them, and re-layouts  38.8 us (9%)
  starting transfers between devices  24.9 us (6%)
  blocking collectives  22.7 us (5%)
  other arithmetic  16.2 us (4%)
  between operations  14.4 us (3%)
    unnamed x6, waiting for transfers between devices  95.5 us
    all_gather x1, waiting for transfers between devices, body(): down_full = lax.all_gather(w_down, 'fsdp', axis=0, tiled=True)  51.3 us
    all_gather x1, waiting for transfers between devices, body(): up_full = lax.all_gather(w_up, 'fsdp', axis=0, tiled=True)  48.2 us
    all_gather x1, blocking collectives, body(): lax.all_gather(jnp.concatenate(small).reshape(1, padded // 128, 128), 'fs...  22.7 us
    all_to_all x1, waiting for transfers between devices, body(): lax.all_to_all(jnp.broadcast_to(grad_mod[None], (owners, own_latents, 6 *...  18.4 us
    all_gather x1, waiting for transfers between devices, body(): out_full = lax.all_gather(w_out, 'fsdp', axis=0, tiled=True)  17.1 us
    all_to_all x1, waiting for transfers between devices, body(): lax.all_to_all(mod_part.reshape(fsdp_count, own_latents * 6 * D), 'fsdp',...  13.7 us
    unnamed x55, local copies, waits for them, and re-layouts  12.7 us
  transfers between devices with their start and end apart: 12, of which 10 were waited for; matrix products, arithmetic and copies ran while one was open for 12% of the time, Pallas kernels for 0%

commit v1 on v0

--- a/solution.py
+++ b/solution.py
@@ -104,8 +104,11 @@
     shift_one, scale_one, gate_one = (mod_parts[:, 0], mod_parts[:, 1], mod_parts[:, 2])
     shift_two, scale_two, gate_two = (mod_parts[:, 3], mod_parts[:, 4], mod_parts[:, 5])
     qkv_full = lax.all_gather(w_qkv, "fsdp", axis=0, tiled=True)
-    out_full = lax.all_gather(w_out, "fsdp", axis=0, tiled=True)
-    up_full = lax.all_gather(w_up, "fsdp", axis=0, tiled=True)
+    out_full, up_full = jnp.split(
+        lax.all_gather(jnp.concatenate([w_out, w_up], axis=1), "fsdp", axis=0, tiled=True),
+        [w_out.shape[1]],
+        axis=1,
+    )
     down_full = lax.all_gather(w_down, "fsdp", axis=0, tiled=True)
     normed_one, inverse_one = normalize(inputs)
     attn_in = (normed_one * (1.0 + scale_one) + shift_one).astype(bf16)

time: 444 us -> 412 us (0.928)
  waiting for transfers between devices: 268 us -> 235 us
    all_gather x1, waiting for transfers between devices: 51.3 us -> 32.3 us  [body(): down_full = lax.all_gather(w_down, 'fsdp', axis=0, tiled=True)]
    all_gather x2 -> x1, waiting for transfers between devices: 65.3 us -> 55.2 us  [body(): lax.all_gather(jnp.concatenate([w_out, w_up], axis=1), 'fsdp', axis=0, ti...]
    unnamed x6 -> x5, waiting for transfers between devices: 95.5 us -> 91.6 us
    unnamed x55 -> x59, local copies, waits for them, and re-layouts: 12.7 us -> 14.8 us
  transfers between devices with their start and end apart: 12 -> 11, of which waited for: 10 -> 9; matrix products, arithmetic and copies ran while one was open for 12% -> 12% of each run, Pallas kernels for 0% -> 0%
where the time goes in v1:
time: 412 us; the launch traced here: 411 us
  waiting for transfers between devices  235 us (57%)
  matrix products  57 us (14%)
  local copies, waits for them, and re-layouts  41.1 us (10%)
  starting transfers between devices  25.3 us (6%)
  blocking collectives  22.7 us (6%)
  other arithmetic  15.7 us (4%)
  between operations  14.4 us (3%)
    unnamed x5, waiting for transfers between devices  91.6 us
    all_gather x1, waiting for transfers between devices, body(): lax.all_gather(jnp.concatenate([w_out, w_up], axis=1), 'fsdp', axis=0, ti...  55.2 us
    all_gather x1, waiting for transfers between devices, body(): down_full = lax.all_gather(w_down, 'fsdp', axis=0, tiled=True)  32.3 us
    all_gather x1, blocking collectives, body(): lax.all_gather(jnp.concatenate(small).reshape(1, padded // 128, 128), 'fs...  22.7 us
    all_to_all x1, waiting for transfers between devices, body(): lax.all_to_all(jnp.broadcast_to(grad_mod[None], (owners, own_latents, 6 *...  18.8 us
    unnamed x59, local copies, waits for them, and re-layouts  14.8 us
    all_to_all x1, waiting for transfers between devices, body(): lax.all_to_all(mod_part.reshape(fsdp_count, own_latents * 6 * D), 'fsdp',...  13.9 us
    all_to_all x1, waiting for transfers between devices, body(): lax.all_to_all(grad_latents, 'sp', split_axis=1, concat_axis=0, tiled=True)  10.5 us
  transfers between devices with their start and end apart: 11, of which 9 were waited for; matrix products, arithmetic and copies ran while one was open for 12% of the time, Pallas kernels for 0%

profile of v1, /device:TPU:0, one launch (start us, length us, event | category | flops | bytes accessed | tf_op | source)
XLA Modules:
  0.0 411.2 jit_solution(12734463641116236920)
XLA Ops:
  8.7 1.7 pad_maximum_fusion.1
  10.5 4.2 %all-to-all-start = ((bf16[2,128,768]{2,1,0:T(8,128)(2,1)}), bf16[2,128,768]{2,1,0:T(8,128)(2,1)S(1)}, u32[]{:S(2)}, u32[]{:S(2)}) async-start(bf16[2,128,768]{2,1,0:T(8,128)(2,1)} %param.14), calls=%async_computation | async-start | bytes 786432 | tf_op jit(solution)/shard_map/all_to_all | solution.py:85
  15.4 4.1 concatenate.27
  19.5 22.7 %all_gather.12 = bf16[16,32,128]{2,1,0:T(8,128)(2,1)S(1)} all-gather(bf16[1,32,128]{2,1,0:T(8,128)(2,1)S(1)} %bitcast.188), channel_id=1, replica_groups=mesh['fsdp'=16,'sp'=2] {'fsdp'}, dimensions={0}, use_global_device_ids=true | all-gather | bytes 139264 | tf_op jit(solution)/shard_map/all_gather | solution.py:74
  44.2 3.5 all-to-all-start.1
  48.5 13.9 %all-to-all-done.1 = f32[16,1,4608]{2,1,0:T(1,128)S(1)} async-done(((f32[16,1,4608]{2,1,0:T(1,128)}), f32[16,1,4608]{2,1,0:T(1,128)S(1)}, u32[]{:S(2)}, u32[]{:S(2)}) %all-to-all-start.1) | async-done | bytes 294944 | tf_op jit(solution)/shard_map/all_to_all | solution.py:95
  62.4 4.0 all-to-all-start.3
  66.7 6.4 %all-to-all-done.3 = bf16[2,128,768]{2,1,0:T(8,128)(2,1)S(1)} async-done(((bf16[2,128,768]{2,1,0:T(8,128)(2,1)}), bf16[2,128,768]{2,1,0:T(8,128)(2,1)S(1)}, u32[]{:S(2)}, u32[]{:S(2)}) %all-to-all-start.3) | async-done | bytes 393248 | tf_op jit(solution)/shard_map/all_to_all | solution.py:86
  74.7 4.2 %fusion.10 = bf16[256,2304]{1,0:T(8,128)(2,1)} fusion(bf16[256,768]{1,0:T(8,128)(2,1)S(1)} %fusion.43, bf16[768,2304]{1,0:T(8,128)(2,1)} %all-gather.4.cloned.1.call-done, f32[2304]{0:T(1024)S(1)} %maximum_convert_fusion), kind=kOutput, calls=%fused_computation.15 | convolution fusion | flops 907149312 | bytes 5121024 | tf_op jit(solution)/shard_map/btd,de->bte/dot_general | solution.py:117
  78.9 1.6 copy.105
  80.5 2.3 fusion.69
  82.7 4.8 %convolution_convert_fusion.4 = bf16[12,256,64]{1,2,0:T(8,128)(2,1)} fusion(f32[12,256,256]{1,2,0:T(8,128)} %fusion.69, bf16[3,1,12,256,64]{3,4,2,1,0:T(8,128)(2,1)S(1)} %bitcast.156), kind=kOutput, calls=%fused_computation.38 | convolution fusion | flops 104008960 | bytes 7077888 | tf_op jit(solution)/shard_map/bhqk,bhkd->bhqd/dot_general | solution.py:127
  87.5 32.3 %all-gather.8.cloned.1.call-done = bf16[3072,768]{1,0:T(8,128)(2,1)} async-done(((bf16[192,768]{1,0:T(8,128)(2,1)}), bf16[3072,768]{1,0:T(8,128)(2,1)}) %all-gather.8.cloned.1.call-update) | async-done | bytes 4718608 | tf_op jit(solution)/shard_map/all_gather | solution.py:112
  119.8 5.5 %fusion.95 = f32[256,3072]{1,0:T(8,128)} fusion(bf16[256,768]{1,0:T(8,128)(2,1)S(1)} %fusion.33, bf16[3072,768]{1,0:T(8,128)(2,1)} %all-gather.8.cloned.1.call-done), kind=kOutput, calls=%fused_computation.166 | convolution fusion | flops 1207959552 | bytes 8257536 | tf_op jit(solution)/shard_map/btd,fd->btf/dot_general | solution.py:150
  125.3 55.2 %all-gather.6.cloned.1.call-done = bf16[768,3840]{1,0:T(8,128)(2,1)} async-done(((bf16[48,3840]{1,0:T(8,128)(2,1)}), bf16[768,3840]{1,0:T(8,128)(2,1)}) %all-gather.6.cloned.1.call-update) | async-done | bytes 5898256 | tf_op jit(solution)/shard_map/all_gather | solution.py:108
  180.6 2.9 fusion.92
  183.8 5.5 %fusion.89 = (bf16[3072]{0:T(1024)(128)(2,1)S(1)}, bf16[256,3072]{1,0:T(8,128)(2,1)S(1)}, f32[256,3072]{1,0:T(8,128)S(1)}) fusion(f32[256,3072]{1,0:T(8,128)S(1)} %copy-done.3, f32[3072]{0:T(1024)S(1)} %reshape.760, bf16[768,3840]{1,0:T(8,128)(2,1)} %all-gather.6.cloned.1.call-done, f32[256,768]{1,0:T(8,128)S(1)} %get-tuple-element.36, ...), kind=kOutput, calls=%fused_computation.160 | convolution fusion | flops 1226241024 | bytes 13395968 | tf_op jit(solution)/shard_map/btd,df->btf/dot_general | solution.py:137
  189.4 4.5 %convolution_convert_fusion.2 = bf16[3072,768]{1,0:T(8,128)(2,1)} fusion(bf16[256,768]{1,0:T(8,128)(2,1)S(1)} %copy-done.7, f32[256,3072]{1,0:T(8,128)S(1)} %get-tuple-element.60), kind=kOutput, calls=%fused_computation.5 | convolution fusion | flops 1217396736 | bytes 8257536 | tf_op jit(solution)/shard_map/btf,btd->fd/dot_general | solution.py:148
  193.9 1.4 fusion.3
  195.3 3.0 fusion.34
  198.3 1.3 fusion.91
  200.3 1.3 convolution_convert_fusion.6
  201.6 1.2 copy.109
  202.7 4.7 %fusion.27 = bf16[1,1,12,256,64]{3,4,2,1,0:T(8,128)(2,1)} fusion(bf16[12,256,64]{1,2,0:T(8,128)(2,1)S(1)} %bitcast.172, f32[12,256,256]{1,2,0:T(8,128)} %fusion.69), kind=kOutput, calls=%fused_computation.43 | convolution fusion | flops 104008960 | bytes 3932160 | tf_op jit(solution)/shard_map/bhqk,bhqd->bhkd/dot_general | solution.py:177
  208.1 1.3 copy-done.1
  209.4 2.6 multiply_reduce_fusion
  212.6 1.3 fusion.29
  214.0 1.1 fusion.28
  215.3 4.7 %copy.117 = bf16[32,24,4,768]{3,2,1,0:T(4,128)(2,1)S(1)} copy(bf16[32,24,4,768]{3,1,2,0:T(8,128)(2,1)} %bitcast.163) | data formatting | bytes 9437184 | tf_op jit(solution)/shard_map/transpose | solution.py:222
  220.0 3.2 copy.132
  224.3 5.0 %constant_dynamic-update-slice_fusion.7 = bf16[768,9344]{1,0:T(8,128)(2,1)} fusion(bf16[768,3072]{1,0:T(8,128)(2,1)} %bitcast.153), kind=kLoop, calls=%fused_computation.116 | loop fusion | bytes 9437184
  229.2 3.8 fusion.2
  233.0 3.0 fusion.1
  236.0 1.5 fusion.24
  240.3 3.0 reduce.65
  244.2 3.7 all-to-all-start.2
  248.0 3.8 fusion.48
  252.2 1.7 copy.113
  254.9 3.6 all-to-all-start.4
  258.6 10.5 %all-to-all-done.4 = f32[1,256,768]{2,0,1:T(1,128)S(1)} async-done(((f32[1,256,768]{2,0,1:T(1,128)}), f32[1,256,768]{2,0,1:T(1,128)S(1)}, u32[]{:S(2)}, u32[]{:S(2)}) %all-to-all-start.4) | async-done | bytes 786464 | tf_op jit(solution)/shard_map/all_to_all | solution.py:193
  270.2 2.6 all-to-all-start.5
  275.4 18.8 %all-to-all-done.5 = f32[32,1,4608]{2,1,0:T(1,128)S(1)} async-done(((f32[32,1,4608]{2,1,0:T(1,128)}), f32[32,1,4608]{2,1,0:T(1,128)S(1)}, u32[]{:S(2)}, u32[]{:S(2)}) %all-to-all-start.5) | async-done | bytes 589856 | tf_op jit(solution)/shard_map/all_to_all | solution.py:205
  295.1 3.5 all-to-all-start.6
  299.0 1.3 fusion.55
  300.9 5.3 %all-to-all-done.6 = f32[16,1,96]{2,1,0:T(1,128)S(1)} async-done(((f32[16,1,96]{2,1,0:T(1,128)}), f32[16,1,96]{2,1,0:T(1,128)S(1)}, u32[]{:S(2)}, u32[]{:S(2)}) %all-to-all-start.6) | async-done | bytes 6176 | tf_op jit(solution)/shard_map/all_to_all | solution.py:259
  308.2 90.2 %reduce-scatter.4.cloned.1.call-done = bf16[24,9344]{1,0:T(8,128)(2,1)} async-done(((bf16[768,9344]{1,0:T(8,128)(2,1)}), bf16[24,9344]{1,0:T(8,128)(2,1)}) %reduce-scatter.4.cloned.1.call-update) | async-done | bytes 448528
  398.3 1.1 convert_element_type.313
  400.7 1.7 fusion.93
  (148 shorter events, 26.2 us)
Async XLA Ops:
  7.2 35.7 %copy-start = (bf16[48,4608]{1,0:T(8,128)(2,1)S(1)}, bf16[48,4608]{1,0:T(8,128)(2,1)}, u32[]{:S(2)}) copy-start(bf16[48,4608]{1,0:T(8,128)(2,1)} %param.17) | copy-start | bytes 1327108
  7.2 67.5 %all-gather.4.cloned.1.call-start = ((), (), s32[]{:S(2)}) async-start(), calls=%async_computation.8 | async-start | bytes 3760128 | tf_op jit(solution)/shard_map/all_gather | solution.py:106
  7.9 111.9 %all-gather.8.cloned.1.call-start = ((), (), s32[]{:S(2)}) async-start(), calls=%async_computation.10 | async-start | bytes 5013504 | tf_op jit(solution)/shard_map/all_gather | solution.py:112
  8.7 171.9 %all-gather.6.cloned.1.call-start = ((), (), s32[]{:S(2)}) async-start(), calls=%async_computation.9 | async-start | bytes 6266880 | tf_op jit(solution)/shard_map/all_gather | solution.py:108
  10.5 33.7 %all-to-all-start = ((bf16[2,128,768]{2,1,0:T(8,128)(2,1)}), bf16[2,128,768]{2,1,0:T(8,128)(2,1)S(1)}, u32[]{:S(2)}, u32[]{:S(2)}) async-start(bf16[2,128,768]{2,1,0:T(8,128)(2,1)} %param.14), calls=%async_computation | async-start | bytes 786432 | tf_op jit(solution)/shard_map/all_to_all | solution.py:85
  44.2 18.2 %all-to-all-start.1 = ((f32[16,1,4608]{2,1,0:T(1,128)}), f32[16,1,4608]{2,1,0:T(1,128)S(1)}, u32[]{:S(2)}, u32[]{:S(2)}) async-start(f32[16,1,4608]{2,1,0:T(1,128)} %copy.104), calls=%async_computation.1 | async-start | bytes 589824 | tf_op jit(solution)/shard_map/all_to_all | solution.py:95
  62.4 10.7 %all-to-all-start.3 = ((bf16[2,128,768]{2,1,0:T(8,128)(2,1)}), bf16[2,128,768]{2,1,0:T(8,128)(2,1)S(1)}, u32[]{:S(2)}, u32[]{:S(2)}) async-start(bf16[2,128,768]{2,1,0:T(8,128)(2,1)} %param.16), calls=%async_computation.3 | async-start | bytes 786432 | tf_op jit(solution)/shard_map/all_to_all | solution.py:86
  66.4 332.0 %reduce-scatter.4.cloned.1.call-start = ((), (), s32[]{:S(2)}) async-start(), calls=%async_computation.11 | async-start | bytes 14800896
  73.4 46.5 %copy-start.6 = (bf16[256,768]{1,0:T(8,128)(2,1)}, bf16[256,768]{1,0:T(8,128)(2,1)S(1)}, u32[]{:S(2)}) copy-start(bf16[256,768]{1,0:T(8,128)(2,1)S(1)} %fusion.33) | copy-start | bytes 1179652
  180.6 3.2 copy-start.3
  183.5 10.3 %slice-start.2 = ((s8[5898240]{0:T(1024)(128)(4,1)}), s8[4194304]{0:T(1024)(128)(4,1)S(1)}, s32[]{:S(2)}) async-start(s8[5898240]{0:T(1024)(128)(4,1)} %bitcast.184), calls=%async_computation.14 | async-start | bytes 8388608
  183.8 5.6 %copy-start.7 = (bf16[256,768]{1,0:T(8,128)(2,1)S(1)}, bf16[256,768]{1,0:T(8,128)(2,1)}, u32[]{:S(2)}) copy-start(bf16[256,768]{1,0:T(8,128)(2,1)} %copy-done.6) | copy-start | bytes 1179652
  183.8 10.1 %slice-start.3 = ((s8[5898240]{0:T(1024)(128)(4,1)}), s8[1703936]{0:T(1024)(128)(4,1)S(1)}, s32[]{:S(2)}) async-start(s8[5898240]{0:T(1024)(128)(4,1)} %bitcast.184), calls=%async_computation.15 | async-start | bytes 3407872
  183.8 11.5 %slice-start = ((s8[4718592]{0:T(1024)(128)(4,1)}), s8[4194304]{0:T(1024)(128)(4,1)S(1)}, s32[]{:S(2)}) async-start(s8[4718592]{0:T(1024)(128)(4,1)} %bitcast.164), calls=%async_computation.12 | async-start | bytes 8388608
  189.3 4.5 %copy-start.17 = (bf16[256,3072]{1,0:T(8,128)(2,1)}, bf16[256,3072]{1,0:T(8,128)(2,1)S(1)}, u32[]{:S(2)}) copy-start(bf16[256,3072]{1,0:T(8,128)(2,1)S(1)} %get-tuple-element.31) | copy-start | bytes 4718596
  189.4 5.9 %slice-start.1 = ((s8[4718592]{0:T(1024)(128)(4,1)}), s8[524288]{0:T(1024)(128)(4,1)S(1)}, s32[]{:S(2)}) async-start(s8[4718592]{0:T(1024)(128)(4,1)} %bitcast.164), calls=%async_computation.13 | async-start | bytes 1048576
  199.5 0.8 copy-start.11
  207.5 1.9 copy-start.1
  220.0 3.2 copy-start.8
  220.0 3.2 copy-start.9
  220.0 3.2 copy-start.13
  224.2 5.0 %copy-start.18 = (bf16[256,3072]{1,0:T(8,128)(2,1)S(1)}, bf16[256,3072]{1,0:T(8,128)(2,1)}, u32[]{:S(2)}) copy-start(bf16[256,3072]{1,0:T(8,128)(2,1)} %copy-done.17) | copy-start | bytes 4718596
  229.2 3.8 copy-start.14
  233.0 3.0 copy-start.10
  233.0 3.0 copy-start.12
  238.2 1.0 copy-start.15
  244.2 10.8 %all-to-all-start.2 = ((bf16[2,2,49152]{2,1,0:T(2,128)(2,1)}), bf16[2,2,49152]{2,1,0:T(2,128)(2,1)S(1)}, u32[]{:S(2)}, u32[]{:S(2)}) async-start(bf16[2,2,49152]{2,1,0:T(2,128)(2,1)} %reshape.781), calls=%async_computation.2 | async-start | bytes 786432 | tf_op jit(solution)/shard_map/all_to_all | solution.py:145
  247.9 3.9 copy-start.4
  247.9 3.9 copy-start.5
  254.9 14.2 %all-to-all-start.4 = ((f32[1,256,768]{2,0,1:T(1,128)}), f32[1,256,768]{2,0,1:T(1,128)S(1)}, u32[]{:S(2)}, u32[]{:S(2)}) async-start(f32[1,256,768]{2,0,1:T(1,128)} %copy.113), calls=%async_computation.4 | async-start | bytes 1572864 | tf_op jit(solution)/shard_map/all_to_all | solution.py:193
  270.2 23.9 %all-to-all-start.5 = ((f32[32,1,4608]{2,1,0:T(1,128)}), f32[32,1,4608]{2,1,0:T(1,128)S(1)}, u32[]{:S(2)}, u32[]{:S(2)}) async-start(f32[32,1,4608]{2,1,0:T(1,128)} %broadcast_in_dim.11), calls=%async_computation.5 | async-start | bytes 1179648 | tf_op jit(solution)/shard_map/all_to_all | solution.py:205
  273.3 34.3 %copy-start.16 = (bf16[2,768]{1,0:T(2,128)(2,1)S(1)}, bf16[2,768]{1,0:T(2,128)(2,1)}, u32[]{:S(2)}) copy-start(bf16[2,768]{1,0:T(2,128)(2,1)} %param.15) | copy-start | bytes 9220
  295.1 11.1 %all-to-all-start.6 = ((f32[16,1,96]{2,1,0:T(1,128)}), f32[16,1,96]{2,1,0:T(1,128)S(1)}, u32[]{:S(2)}, u32[]{:S(2)}) async-start(f32[16,1,96]{2,1,0:T(1,128)} %bitcast.29), calls=%async_computation.6 | async-start | bytes 16384 | tf_op jit(solution)/shard_map/all_to_all | solution.py:259
  398.3 5.0 %copy-start.2 = (bf16[24,9344]{1,0:T(8,128)(2,1)S(1)}, bf16[24,9344]{1,0:T(8,128)(2,1)}, u32[]{:S(2)}) copy-start(bf16[24,9344]{1,0:T(8,128)(2,1)} %reduce-scatter.4.cloned.1.call-done) | copy-start | bytes 1345540
Sparse Core Ops, SparseCore 0:
  10.3 55.5 all-gather.3
  68.2 51.5 all-gather.7
  122.7 57.8 all-gather.5
  238.3 159.9 reduce-scatter.3
